TPU v7x, 32 devices: a whole 2x2x4 slice. The times are simulated.
32 devices in a mesh: wide: 8 (over y, x, core), blk: 4 (over z).
Axes of the slice: x: 2, y: 2, z: 4, core: 2. Of those that a mesh axis runs over, the one named last changes fastest.
Arguments:
- audio: bfloat16 [4096, 1024], P(('wide', 'blk')), may hold values from -1 to 1
- video: bfloat16 [4096, 1024], P(('wide', 'blk')), may hold values from -1 to 1
- owner: int32 [4096, 1], P(('wide', 'blk')), may hold values from 0 to 7; in each aligned block of 128 rows (0 to 127, 128 to 255, ...) at most 32 rows name the same one
- clip_feats: bfloat16 [8192, 1024], P(('wide', 'blk')), may hold values from -24 to 24
- lengths: int32 [8192], P(('wide', 'blk')), may hold values from 1 to 16
- proj_weight: bfloat16 [1024, 1024], replicated, may hold values from -0.1875 to 0.1875
Outputs:
- audio_grad: bfloat16 [4096, 1024], P(('wide', 'blk'))
- feats_grad: bfloat16 [8192, 1024], P(('wide', 'blk'))
- weight_grad: float32 [1024, 1024], P('wide')
Inputs may be any that keep to these rules, and one draw needn't show every extreme that they name: Among the 128 rows of one device, no owner is named more than 32 times, a bound that some block reaches.
All inputs are finite; a program needn't handle non-finite values.
Results may differ from a plain program's by a relative error of at most 0.02.
Values may be sent and summed in bfloat16 or wider, within the bound.
A program may use at most 64 MiB of HBM per device.

v0:
```python
from functools import partial
import jax
import jax.numpy as jnp
from jax import lax
from jax.sharding import PartitionSpec as P


def rows_dot(matrix_a, matrix_b):
    return lax.dot_general(
        matrix_a, matrix_b, (((1,), (1,)), ((), ())), preferred_element_type=jnp.float32
    )


def cols_dot(matrix_a, matrix_b):
    return lax.dot_general(
        matrix_a, matrix_b, (((0,), (0,)), ((), ())), preferred_element_type=jnp.float32
    )


def pair_coeffs(scores, labels, factor):
    return (factor * (jax.nn.sigmoid(4.0 * scores - 2.0) - labels)).astype(jnp.bfloat16)


def shards(audio, video, owner, clip_feats, lengths, proj_weight):
    blocks = lax.axis_size("blk")
    clip_count = audio.shape[0]
    feature_count = audio.shape[1]
    factor = 4.0 / blocks
    row_ids = jnp.arange(clip_count, dtype=jnp.int32)
    offset = lax.axis_index("blk") * clip_count
    gathered = lax.all_gather(video, "blk", axis=0, tiled=True)
    other_ids = jnp.arange(gathered.shape[0], dtype=jnp.int32)
    labels = ((offset + row_ids)[:, None] == other_ids[None, :]).astype(jnp.float32)
    coeffs = pair_coeffs(rows_dot(audio, gathered), labels, factor)
    audio_total = jnp.dot(coeffs, gathered, preferred_element_type=jnp.float32)
    gathered = lax.all_gather(audio, "blk", axis=0, tiled=True)
    other_ids = jnp.arange(gathered.shape[0], dtype=jnp.int32)
    labels = (other_ids[:, None] == (offset + row_ids)[None, :]).astype(jnp.float32)
    coeffs = pair_coeffs(rows_dot(gathered, video), labels, factor)
    video_sum = cols_dot(coeffs, gathered)
    audio_grad = audio_total.astype(jnp.bfloat16)
    video_grad = video_sum.astype(jnp.bfloat16)
    peer_count = lax.axis_size("wide")
    slot_count = clip_feats.shape[0]
    capacity = slot_count // peer_count
    owner_peer = owner[:, 0]
    onehot = (owner_peer[:, None] == jnp.arange(peer_count, dtype=jnp.int32)[None, :]).astype(
        jnp.int32
    )
    slot_rank = jnp.sum((jnp.cumsum(onehot, axis=0) - onehot) * onehot, axis=1)
    target = owner_peer * capacity + slot_rank
    placing = (jnp.arange(slot_count, dtype=jnp.int32)[:, None] == target[None, :]).astype(
        jnp.bfloat16
    )
    packed = jnp.dot(placing, video_grad, preferred_element_type=jnp.float32).astype(jnp.bfloat16)
    packed = packed.reshape(peer_count, capacity, feature_count)
    received = lax.all_to_all(packed, "wide", split_axis=0, concat_axis=0, tiled=True).reshape(
        slot_count, feature_count
    )
    length_scale = lax.rsqrt(lengths.astype(jnp.float32))[:, None]
    pooled = (clip_feats.astype(jnp.float32) * length_scale).astype(jnp.bfloat16)
    preact = jnp.dot(pooled, proj_weight, preferred_element_type=jnp.float32)
    _, pullback = jax.vjp(partial(jax.nn.gelu, approximate=False), preact)
    pre_grad = pullback(received.astype(jnp.float32))[0].astype(jnp.bfloat16)
    feats_grad = (rows_dot(pre_grad, proj_weight) * length_scale).astype(jnp.bfloat16)
    partial_rows = lax.psum_scatter(
        cols_dot(pooled, pre_grad).astype(jnp.bfloat16), "wide", scatter_dimension=0, tiled=True
    )
    weight_grad = lax.psum(partial_rows, "blk").astype(jnp.float32)
    return (audio_grad, feats_grad, weight_grad)


def solution(mesh):
    return jax.shard_map(
        shards,
        mesh=mesh,
        in_specs=(
            P(("wide", "blk"), None),
            P(("wide", "blk"), None),
            P(("wide", "blk"), None),
            P(("wide", "blk"), None),
            P(("wide", "blk")),
            P(),
        ),
        out_specs=(P(("wide", "blk"), None), P(("wide", "blk"), None), P("wide", None)),
        check_vma=False,
    )
```

profile of v0, /device:TPU:0, one launch (start us, length us, event | category | flops | bytes accessed | tf_op | source)
XLA Modules:
  0.0 167.4 jit_solution(1915806834253951210)
XLA Ops:
  7.2 0.0 copy-start
  7.2 0.0 all-gather.5.cloned.1.call-start
  7.2 0.7 all-gather.5.cloned.1.call-update
  7.9 0.7 fusion.37
  8.7 0.2 reduce_window_sum.11
  8.8 0.8 select_reduce_fusion
  9.7 0.7 multiply_add_fusion
  10.3 30.0 %all-gather.5.cloned.1.call-done = bf16[512,1024]{1,0:T(8,128)(2,1)} async-done(((bf16[128,1024]{1,0:T(8,128)(2,1)}), bf16[512,1024]{1,0:T(8,128)(2,1)}) %all-gather.5.cloned.1.call-update) | async-done | bytes 1048592 | tf_op jit(solution)/shard_map/all_gather | solution.py:36
  40.3 0.0 copy-start.1
  40.3 1.8 %fusion.14 = bf16[512,128]{1,0:T(8,128)(2,1)S(1)} fusion(bf16[512,1024]{1,0:T(8,128)(2,1)} %all-gather.5.cloned.1.call-done, bf16[128,1024]{1,0:T(8,128)(2,1)} %param.7, s32[128]{0:T(128)S(1)} %iota_add_fusion), kind=kOutput, calls=%fused_computation.24 | convolution fusion | flops 134807552 | bytes 1442304 | tf_op jit(solution)/shard_map/dot_general | solution.py:9
  42.1 0.0 copy-done.1
  42.1 0.0 copy-start.6
  42.1 1.4 convolution_convert_fusion.1
  43.5 3.7 %all-to-all-start = ((bf16[8,32,1024]{2,1,0:T(8,128)(2,1)}), bf16[8,32,1024]{2,1,0:T(8,128)(2,1)S(1)}, u32[]{:S(2)}, u32[]{:S(2)}) async-start(bf16[8,32,1024]{2,1,0:T(8,128)(2,1)} %bitcast.1), calls=%async_computation | async-start | bytes 1048576 | tf_op jit(solution)/shard_map/all_to_all | solution.py:57
  47.2 0.0 all-gather.3.cloned.1.call-start
  47.2 0.7 all-gather.3.cloned.1.call-update
  47.9 0.0 reduce-scatter.2.cloned.1.call-start
  48.0 0.0 copy-done.6
  48.0 0.0 copy-start.2
  48.0 8.9 %all-to-all-done = bf16[8,32,1024]{2,1,0:T(8,128)(2,1)S(1)} async-done(((bf16[8,32,1024]{2,1,0:T(8,128)(2,1)}), bf16[8,32,1024]{2,1,0:T(8,128)(2,1)S(1)}, u32[]{:S(2)}, u32[]{:S(2)}) %all-to-all-start) | async-done | bytes 524320 | tf_op jit(solution)/shard_map/all_to_all | solution.py:57
  56.9 0.0 copy-done
  56.9 4.2 %fusion.20 = bf16[256,1024]{1,0:T(8,128)(2,1)S(1)} fusion(bf16[8,32,1024]{2,1,0:T(8,128)(2,1)S(1)} %all-to-all-done, bf16[1024,1024]{1,0:T(8,128)(2,1)S(1)} %copy-done, bf16[256,1024]{1,0:T(8,128)(2,1)} %param.9, f32[256]{0:T(256)S(1)} %convert_rsqrt_fusion), kind=kOutput, calls=%fused_computation.30 | convolution fusion | flops 556793856 | bytes 3671040 | tf_op jit(solution)/shard_map/dot_general | solution.py:62
  61.1 0.0 copy-start.3
  61.1 0.8 copy-done.3
  61.9 0.0 copy-done.2
  61.9 0.0 copy-start.5
  61.9 2.2 %convolution_convert_fusion = bf16[1024,1024]{1,0:T(8,128)(2,1)} fusion(bf16[256,1024]{1,0:T(8,128)(2,1)S(1)} %fusion.20, bf16[256,1024]{1,0:T(8,128)(2,1)S(1)} %copy-done.2, f32[256]{0:T(256)S(1)} %convert_rsqrt_fusion), kind=kOutput, calls=%fused_computation | convolution fusion | flops 538705920 | bytes 3146752 | tf_op jit(solution)/shard_map/dot_general | solution.py:15
  64.1 0.0 reduce-scatter.2.cloned.1.call-update
  64.1 0.0 copy-start.4
  64.1 0.0 all-reduce.2.cloned.1.call-start
  64.2 13.3 %all-gather.3.cloned.1.call-done = bf16[512,1024]{1,0:T(8,128)(2,1)} async-done(((bf16[128,1024]{1,0:T(8,128)(2,1)}), bf16[512,1024]{1,0:T(8,128)(2,1)}) %all-gather.3.cloned.1.call-update) | async-done | bytes 1048592 | tf_op jit(solution)/shard_map/all_gather | solution.py:31
  77.5 0.0 copy-done.5
  77.5 3.1 %convolution_convert_fusion.3 = bf16[128,1024]{1,0:T(8,128)(2,1)} fusion(bf16[512,1024]{1,0:T(8,128)(2,1)} %all-gather.3.cloned.1.call-done, bf16[128,1024]{1,0:T(8,128)(2,1)S(1)} %copy-done.5, s32[128]{0:T(128)S(1)} %iota_add_fusion), kind=kOutput, calls=%fused_computation.8 | convolution fusion | flops 269156352 | bytes 1573376 | tf_op jit(solution)/shard_map/dot_general | solution.py:35
  80.5 40.8 %reduce-scatter.2.cloned.1.call-done = bf16[128,1024]{1,0:T(8,128)(2,1)} async-done(((bf16[1024,1024]{1,0:T(8,128)(2,1)}), bf16[128,1024]{1,0:T(8,128)(2,1)}) %reduce-scatter.2.cloned.1.call-update) | async-done | bytes 262160 | tf_op jit(solution)/shard_map/reduce_scatter | solution.py:66
  121.3 0.0 all-reduce.2.cloned.1.call-update
  121.3 0.0 copy-done.4
  121.3 1.6 fusion
  122.9 36.2 %all-reduce.2.cloned.1.call-done = bf16[128,1024]{1,0:T(8,128)(2,1)} async-done(((bf16[128,1024]{1,0:T(8,128)(2,1)}), bf16[128,1024]{1,0:T(8,128)(2,1)}) %all-reduce.2.cloned.1.call-update) | async-done | bytes 262160 | tf_op jit(solution)/shard_map/psum | solution.py:69
  159.1 1.8 %convert_element_type.68 = f32[128,1024]{1,0:T(8,128)} convert(bf16[128,1024]{1,0:T(8,128)(2,1)} %all-reduce.2.cloned.1.call-done) | non-fusion elementwise | flops 131072 | bytes 786432 | tf_op jit(solution)/shard_map/convert_element_type | solution.py:69
  (2 shorter events, 0.0 us)
Async XLA Ops:
  7.2 49.7 %copy-start = (bf16[1024,1024]{1,0:T(8,128)(2,1)S(1)}, bf16[1024,1024]{1,0:T(8,128)(2,1)}, u32[]{:S(2)}) copy-start(bf16[1024,1024]{1,0:T(8,128)(2,1)} %param.11) | copy-start | bytes 6291460
  7.2 33.1 %all-gather.5.cloned.1.call-start = ((), (), s32[]{:S(2)}) async-start(), calls=%async_computation.3 | async-start | bytes 1310720 | tf_op jit(solution)/shard_map/all_gather | solution.py:36
  40.3 1.8 %copy-start.1 = (bf16[512,1024]{1,0:T(8,128)(2,1)S(1)}, bf16[512,1024]{1,0:T(8,128)(2,1)}, u32[]{:S(2)}) copy-start(bf16[512,1024]{1,0:T(8,128)(2,1)} %all-gather.5.cloned.1.call-done) | copy-start | bytes 3145732
  42.1 5.8 %copy-start.6 = (s32[256]{0:T(256)S(1)}, s32[256]{0:T(256)}, u32[]{:S(2)}) copy-start(s32[256]{0:T(256)} %param.10) | copy-start | bytes 3076
  43.5 13.4 %all-to-all-start = ((bf16[8,32,1024]{2,1,0:T(8,128)(2,1)}), bf16[8,32,1024]{2,1,0:T(8,128)(2,1)S(1)}, u32[]{:S(2)}, u32[]{:S(2)}) async-start(bf16[8,32,1024]{2,1,0:T(8,128)(2,1)} %bitcast.1), calls=%async_computation | async-start | bytes 1048576 | tf_op jit(solution)/shard_map/all_to_all | solution.py:57
  47.2 30.3 %all-gather.3.cloned.1.call-start = ((), (), s32[]{:S(2)}) async-start(), calls=%async_computation.2 | async-start | bytes 1310720 | tf_op jit(solution)/shard_map/all_gather | solution.py:31
  47.9 73.4 %reduce-scatter.2.cloned.1.call-start = ((), (), s32[]{:S(2)}) async-start(), calls=%async_computation.4 | async-start | bytes 2359296 | tf_op jit(solution)/shard_map/reduce_scatter | solution.py:66
  48.0 13.9 %copy-start.2 = (bf16[256,1024]{1,0:T(8,128)(2,1)S(1)}, bf16[256,1024]{1,0:T(8,128)(2,1)}, u32[]{:S(2)}) copy-start(bf16[256,1024]{1,0:T(8,128)(2,1)} %param.9) | copy-start | bytes 1572868
  61.1 0.8 copy-start.3
  61.9 15.6 %copy-start.5 = (bf16[128,1024]{1,0:T(8,128)(2,1)S(1)}, bf16[128,1024]{1,0:T(8,128)(2,1)}, u32[]{:S(2)}) copy-start(bf16[128,1024]{1,0:T(8,128)(2,1)} %param.6) | copy-start | bytes 786436
  64.1 57.2 %copy-start.4 = (bf16[256,1024]{1,0:T(8,128)(2,1)S(1)}, bf16[256,1024]{1,0:T(8,128)(2,1)}, u32[]{:S(2)}) copy-start(bf16[256,1024]{1,0:T(8,128)(2,1)} %copy-done.3) | copy-start | bytes 1572868
  64.1 95.0 %all-reduce.2.cloned.1.call-start = ((), (), s32[]{:S(2)}) async-start(), calls=%async_computation.5 | async-start | bytes 524288 | tf_op jit(solution)/shard_map/psum | solution.py:69
Sparse Core Ops, SparseCore 0:
  9.6 30.6 all-gather.4
  49.5 27.8 all-gather.2
  80.7 40.4 reduce-scatter.1
  123.5 35.5 all-reduce.1
where the time goes:
time: 168 us; the launch traced here: 167 us
  waiting for transfers between devices  131 us (78%)
  matrix products  14.2 us (8%)
  between operations  13.9 us (8%)
  other arithmetic  4.2 us (2%)
  starting transfers between devices  3.81 us (2%)
    reduce_scatter x1, waiting for transfers between devices, shards(): lax.psum_scatter(cols_dot(pooled, pre_grad).astype(jnp.bfloat16), 'wide',...  40.8 us
    psum x1, waiting for transfers between devices, shards(): weight_grad = lax.psum(partial_rows, 'blk').astype(jnp.float32)  36.2 us
    all_gather x1, waiting for transfers between devices, shards(): gathered = lax.all_gather(audio, 'blk', axis=0, tiled=True)  30 us
    all_gather x1, waiting for transfers between devices, shards(): gathered = lax.all_gather(video, 'blk', axis=0, tiled=True)  13.3 us
    all_to_all x1, waiting for transfers between devices, shards(): lax.all_to_all(packed, 'wide', split_axis=0, concat_axis=0, tiled=True)  8.88 us
    dot_general x1, matrix products, shards(): preact = jnp.dot(pooled, proj_weight, preferred_element_type=jnp.float32)  4.22 us
    all_to_all x1, starting transfers between devices, shards(): lax.all_to_all(packed, 'wide', split_axis=0, concat_axis=0, tiled=True)  3.65 us
    dot_general x2, matrix products, rows_dot(): lax.dot_general(matrix_a, matrix_b, (((1,), (1,)), ((), ())), preferred_e...  3.41 us
  transfers between devices with their start and end apart: 5, of which 5 were waited for; matrix products, arithmetic and copies ran while one was open for 8% of the time, Pallas kernels for 0%

commit v1 on v0

--- a/solution.py
+++ b/solution.py
@@ -3,6 +3,16 @@
 import jax.numpy as jnp
 from jax import lax
 from jax.sharding import PartitionSpec as P
+
+
+def around_the_ring(x, name, dim):
+    count = lax.axis_size(name)
+    held, pieces = (x, [x])
+    for _ in range(count - 1):
+        held = lax.ppermute(held, name, [(i, (i + 1) % count) for i in range(count)])
+        pieces.insert(0, held)
+    merged = jnp.concatenate(pieces, axis=dim)
+    return jnp.roll(merged, (lax.axis_index(name) + 1) * x.shape[dim], axis=dim)
 
 
 def rows_dot(matrix_a, matrix_b):
@@ -28,7 +38,7 @@
     factor = 4.0 / blocks
     row_ids = jnp.arange(clip_count, dtype=jnp.int32)
     offset = lax.axis_index("blk") * clip_count
-    gathered = lax.all_gather(video, "blk", axis=0, tiled=True)
+    gathered = around_the_ring(video, "blk", 0)
     other_ids = jnp.arange(gathered.shape[0], dtype=jnp.int32)
     labels = ((offset + row_ids)[:, None] == other_ids[None, :]).astype(jnp.float32)
     coeffs = pair_coeffs(rows_dot(audio, gathered), labels, factor)

time: 168 us -> 149 us (0.89)
  waiting for transfers between devices: 131 us -> 105 us
  local copies, waits for them, and re-layouts: 0.82 us -> 6.58 us
    reduce_scatter x1, waiting for transfers between devices: 40.8 us -> 4.92 us  [shards(): lax.psum_scatter(cols_dot(pooled, pre_grad).astype(jnp.bfloat16), 'wide',...]
    ppermute x0 -> x3, waiting for transfers between devices: none -> 23.4 us  [around_the_ring(): lax.ppermute(held, name, [(i, (i + 1) % count) for i in range(count)])]
    all_gather x1 -> x0, waiting for transfers between devices: 13.3 us -> none  [shards(): gathered = lax.all_gather(video, 'blk', axis=0, tiled=True)]
    unnamed x14 -> x23, local copies, waits for them, and re-layouts: 0.82 us -> 5.87 us
  transfers between devices with their start and end apart: 5 -> 7, of which waited for: 5 -> 7; matrix products, arithmetic and copies ran while one was open for 8% -> 9% of each run, Pallas kernels for 0% -> 0%
where the time goes in v1:
time: 149 us
  waiting for transfers between devices  105 us (70%)
  matrix products  14.3 us (10%)
  between operations  13.9 us (9%)
  local copies, waits for them, and re-layouts  6.58 us (4%)
  starting transfers between devices  5.27 us (4%)
  other arithmetic  4.2 us (3%)
    psum x1, waiting for transfers between devices, shards(): weight_grad = lax.psum(partial_rows, 'blk').astype(jnp.float32)  36.2 us
    all_gather x1, waiting for transfers between devices, shards(): gathered = lax.all_gather(audio, 'blk', axis=0, tiled=True)  30 us
    ppermute x3, waiting for transfers between devices, around_the_ring(): lax.ppermute(held, name, [(i, (i + 1) % count) for i in range(count)])  23.4 us
    all_to_all x1, waiting for transfers between devices, shards(): lax.all_to_all(packed, 'wide', split_axis=0, concat_axis=0, tiled=True)  9.63 us
    unnamed x23, local copies, waits for them, and re-layouts  5.87 us
    reduce_scatter x1, waiting for transfers between devices, shards(): lax.psum_scatter(cols_dot(pooled, pre_grad).astype(jnp.bfloat16), 'wide',...  4.92 us
    dot_general x1, matrix products, shards(): preact = jnp.dot(pooled, proj_weight, preferred_element_type=jnp.float32)  4.2 us
    all_to_all x1, starting transfers between devices, shards(): lax.all_to_all(packed, 'wide', split_axis=0, concat_axis=0, tiled=True)  3.65 us
  transfers between devices with their start and end apart: 7, of which 7 were waited for; matrix products, arithmetic and copies ran while one was open for 9% of the time, Pallas kernels for 0%

profile of v1, /device:TPU:0, one launch (start us, length us, event | category | flops | bytes accessed | tf_op | source)
XLA Modules:
  0.0 149.0 jit_solution(14570207833803825032)
XLA Ops:
  7.2 0.0 copy-start
  7.2 0.0 all-gather.2.cloned.1.call-start
  7.2 0.7 all-gather.2.cloned.1.call-update
  7.9 0.7 fusion.40
  8.7 0.2 reduce_window_sum.11
  8.8 0.8 select_reduce_fusion
  9.7 0.7 multiply_add_fusion
  10.3 30.0 %all-gather.2.cloned.1.call-done = bf16[512,1024]{1,0:T(8,128)(2,1)} async-done(((bf16[128,1024]{1,0:T(8,128)(2,1)}), bf16[512,1024]{1,0:T(8,128)(2,1)}) %all-gather.2.cloned.1.call-update) | async-done | bytes 1048592 | tf_op jit(solution)/shard_map/all_gather | solution.py:46
  40.3 0.0 copy-start.1
  40.3 1.8 %fusion.15 = bf16[512,128]{1,0:T(8,128)(2,1)S(1)} fusion(bf16[512,1024]{1,0:T(8,128)(2,1)} %all-gather.2.cloned.1.call-done, bf16[128,1024]{1,0:T(8,128)(2,1)} %param.7, s32[128]{0:T(128)S(1)} %iota_add_fusion), kind=kOutput, calls=%fused_computation.25 | convolution fusion | flops 134807552 | bytes 1442304 | tf_op jit(solution)/shard_map/dot_general | solution.py:19
  42.1 0.0 copy-done.1
  42.1 1.4 convolution_convert_fusion.1
  43.5 3.7 %all-to-all-start = ((bf16[8,32,1024]{2,1,0:T(8,128)(2,1)}), bf16[8,32,1024]{2,1,0:T(8,128)(2,1)S(1)}, u32[]{:S(2)}, u32[]{:S(2)}) async-start(bf16[8,32,1024]{2,1,0:T(8,128)(2,1)} %bitcast.2), calls=%async_computation | async-start | bytes 1048576 | tf_op jit(solution)/shard_map/all_to_all | solution.py:67
  47.1 0.0 reduce-scatter.2.cloned.1.call-start
  47.2 0.0 copy-done.7
  47.2 0.0 copy-start.3
  47.2 9.6 %all-to-all-done = bf16[8,32,1024]{2,1,0:T(8,128)(2,1)S(1)} async-done(((bf16[8,32,1024]{2,1,0:T(8,128)(2,1)}), bf16[8,32,1024]{2,1,0:T(8,128)(2,1)S(1)}, u32[]{:S(2)}, u32[]{:S(2)}) %all-to-all-start) | async-done | bytes 524320 | tf_op jit(solution)/shard_map/all_to_all | solution.py:67
  56.9 0.0 copy-done
  56.9 4.2 %fusion.21 = bf16[256,1024]{1,0:T(8,128)(2,1)S(1)} fusion(bf16[8,32,1024]{2,1,0:T(8,128)(2,1)S(1)} %all-to-all-done, bf16[1024,1024]{1,0:T(8,128)(2,1)S(1)} %copy-done, bf16[256,1024]{1,0:T(8,128)(2,1)} %param.9, f32[256]{0:T(256)S(1)} %convert_rsqrt_fusion), kind=kOutput, calls=%fused_computation.31 | convolution fusion | flops 556793856 | bytes 3671040 | tf_op jit(solution)/shard_map/dot_general | solution.py:72
  61.1 0.0 copy-start.4
  61.1 0.8 copy-done.4
  61.9 0.0 copy-done.3
  61.9 2.2 %convolution_convert_fusion = bf16[1024,1024]{1,0:T(8,128)(2,1)} fusion(bf16[256,1024]{1,0:T(8,128)(2,1)S(1)} %fusion.21, bf16[256,1024]{1,0:T(8,128)(2,1)S(1)} %copy-done.3, f32[256]{0:T(256)S(1)} %convert_rsqrt_fusion), kind=kOutput, calls=%fused_computation | convolution fusion | flops 538705920 | bytes 3146752 | tf_op jit(solution)/shard_map/dot_general | solution.py:25
  64.0 0.0 reduce-scatter.2.cloned.1.call-update
  64.1 0.0 all-reduce.2.cloned.1.call-start
  64.1 0.0 copy-done.2
  64.1 1.5 %collective-permute-start = (bf16[128,1024]{1,0:T(8,128)(2,1)S(1)}, bf16[128,1024]{1,0:T(8,128)(2,1)S(1)}, u32[]{:S(2)}, u32[]{:S(2)}) collective-permute-start(bf16[128,1024]{1,0:T(8,128)(2,1)S(1)} %copy-done.2), channel_id=1, source_target_pairs={{0,1},{1,2},{2,3},{3,0},{4,5},{5,6},{6,7},{7,4},{8,9},{9,10},{10,1... | collective-permute-start | bytes 786440 | tf_op jit(solution)/shard_map/ppermute | solution.py:12
  65.6 6.7 %collective-permute-done = bf16[128,1024]{1,0:T(8,128)(2,1)S(1)} collective-permute-done((bf16[128,1024]{1,0:T(8,128)(2,1)S(1)}, bf16[128,1024]{1,0:T(8,128)(2,1)S(1)}, u32[]{:S(2)}, u32[]{:S(2)}) %collective-permute-start) | collective-permute-done | bytes 262176 | tf_op jit(solution)/shard_map/ppermute | solution.py:12
  72.4 0.0 collective-permute-start.1
  72.4 8.5 %collective-permute-done.1 = bf16[128,1024]{1,0:T(8,128)(2,1)S(1)} collective-permute-done((bf16[128,1024]{1,0:T(8,128)(2,1)S(1)}, bf16[128,1024]{1,0:T(8,128)(2,1)S(1)}, u32[]{:S(2)}, u32[]{:S(2)}) %collective-permute-start.1) | collective-permute-done | bytes 262176 | tf_op jit(solution)/shard_map/ppermute | solution.py:12
  80.9 0.0 collective-permute-start.2
  80.9 8.2 %collective-permute-done.2 = bf16[128,1024]{1,0:T(8,128)(2,1)S(1)} collective-permute-done((bf16[128,1024]{1,0:T(8,128)(2,1)S(1)}, bf16[128,1024]{1,0:T(8,128)(2,1)S(1)}, u32[]{:S(2)}, u32[]{:S(2)}) %collective-permute-start.2) | collective-permute-done | bytes 262176 | tf_op jit(solution)/shard_map/ppermute | solution.py:12
  89.0 0.7 constant_dynamic-update-slice_fusion.7
  89.7 0.7 constant_dynamic-update-slice_fusion.6
  90.5 0.7 constant_dynamic-update-slice_fusion.5
  91.2 0.7 constant_dynamic-update-slice_fusion.4
  91.9 0.7 constant_dynamic-update-slice_fusion.3
  92.6 0.7 constant_dynamic-update-slice_fusion.2
  93.3 0.7 constant_dynamic-update-slice_fusion.1
  94.1 0.7 constant_dynamic-update-slice_fusion
  94.8 0.0 copy-done.6
  94.8 3.2 %convolution_convert_fusion.3 = bf16[128,1024]{1,0:T(8,128)(2,1)} fusion(bf16[128,1024]{1,0:T(8,128)(2,1)S(1)} %copy-done.6, bf16[1024,1024]{1,0:T(8,128)(2,1)} %constant_dynamic-update-slice_fusion, s32[]{:T(128)S(6)} %select_n.14, s32[128]{0:T(128)S(1)} %iota_add_fusion), kind=kOutput, calls=%fused_computation.8 | convolution fusion | flops 269156352 | bytes 2622976 | tf_op jit(solution)/shard_map/dot_general | solution.py:45
  98.0 4.9 %reduce-scatter.2.cloned.1.call-done = bf16[128,1024]{1,0:T(8,128)(2,1)} async-done(((bf16[1024,1024]{1,0:T(8,128)(2,1)}), bf16[128,1024]{1,0:T(8,128)(2,1)}) %reduce-scatter.2.cloned.1.call-update) | async-done | bytes 262160 | tf_op jit(solution)/shard_map/reduce_scatter | solution.py:76
  102.9 0.0 all-reduce.2.cloned.1.call-update
  102.9 0.0 copy-done.5
  102.9 1.5 %fusion = bf16[256,1024]{1,0:T(8,128)(2,1)} fusion(bf16[256,1024]{1,0:T(8,128)(2,1)S(1)} %copy-done.5, bf16[1024,1024]{1,0:T(8,128)(2,1)S(1)} %copy-done, f32[256]{0:T(256)S(1)} %convert_rsqrt_fusion), kind=kOutput, calls=%fused_computation.5 | convolution fusion | flops 537395200 | bytes 3146752 | tf_op jit(solution)/shard_map/dot_general | solution.py:19
  104.5 36.2 %all-reduce.2.cloned.1.call-done = bf16[128,1024]{1,0:T(8,128)(2,1)} async-done(((bf16[128,1024]{1,0:T(8,128)(2,1)}), bf16[128,1024]{1,0:T(8,128)(2,1)}) %all-reduce.2.cloned.1.call-update) | async-done | bytes 262160 | tf_op jit(solution)/shard_map/psum | solution.py:79
  140.7 1.8 %convert_element_type.68 = f32[128,1024]{1,0:T(8,128)} convert(bf16[128,1024]{1,0:T(8,128)(2,1)} %all-reduce.2.cloned.1.call-done) | non-fusion elementwise | flops 131072 | bytes 786432 | tf_op jit(solution)/shard_map/convert_element_type | solution.py:79
  (6 shorter events, 0.0 us)
Async XLA Ops:
  7.2 49.7 %copy-start = (bf16[1024,1024]{1,0:T(8,128)(2,1)S(1)}, bf16[1024,1024]{1,0:T(8,128)(2,1)}, u32[]{:S(2)}) copy-start(bf16[1024,1024]{1,0:T(8,128)(2,1)} %param.11) | copy-start | bytes 6291460
  7.2 33.1 %all-gather.2.cloned.1.call-start = ((), (), s32[]{:S(2)}) async-start(), calls=%async_computation.2 | async-start | bytes 1310720 | tf_op jit(solution)/shard_map/all_gather | solution.py:46
  10.3 36.9 %copy-start.7 = (s32[256]{0:T(256)S(1)}, s32[256]{0:T(256)}, u32[]{:S(2)}) copy-start(s32[256]{0:T(256)} %param.10) | copy-start | bytes 3076
  40.3 1.8 %copy-start.1 = (bf16[512,1024]{1,0:T(8,128)(2,1)S(1)}, bf16[512,1024]{1,0:T(8,128)(2,1)}, u32[]{:S(2)}) copy-start(bf16[512,1024]{1,0:T(8,128)(2,1)} %all-gather.2.cloned.1.call-done) | copy-start | bytes 3145732
  43.5 13.4 %all-to-all-start = ((bf16[8,32,1024]{2,1,0:T(8,128)(2,1)}), bf16[8,32,1024]{2,1,0:T(8,128)(2,1)S(1)}, u32[]{:S(2)}, u32[]{:S(2)}) async-start(bf16[8,32,1024]{2,1,0:T(8,128)(2,1)} %bitcast.2), calls=%async_computation | async-start | bytes 1048576 | tf_op jit(solution)/shard_map/all_to_all | solution.py:67
  47.1 55.7 %reduce-scatter.2.cloned.1.call-start = ((), (), s32[]{:S(2)}) async-start(), calls=%async_computation.3 | async-start | bytes 2359296 | tf_op jit(solution)/shard_map/reduce_scatter | solution.py:76
  47.2 14.6 %copy-start.3 = (bf16[256,1024]{1,0:T(8,128)(2,1)S(1)}, bf16[256,1024]{1,0:T(8,128)(2,1)}, u32[]{:S(2)}) copy-start(bf16[256,1024]{1,0:T(8,128)(2,1)} %param.9) | copy-start | bytes 1572868
  61.1 0.8 copy-start.4
  61.9 2.3 %copy-start.2 = (bf16[128,1024]{1,0:T(8,128)(2,1)S(1)}, bf16[128,1024]{1,0:T(8,128)(2,1)}, u32[]{:S(2)}) copy-start(bf16[128,1024]{1,0:T(8,128)(2,1)} %param.7) | copy-start | bytes 786436
  64.1 76.6 %all-reduce.2.cloned.1.call-start = ((), (), s32[]{:S(2)}) async-start(), calls=%async_computation.4 | async-start | bytes 524288 | tf_op jit(solution)/shard_map/psum | solution.py:79
  64.1 8.2 %collective-permute-start = (bf16[128,1024]{1,0:T(8,128)(2,1)S(1)}, bf16[128,1024]{1,0:T(8,128)(2,1)S(1)}, u32[]{:S(2)}, u32[]{:S(2)}) collective-permute-start(bf16[128,1024]{1,0:T(8,128)(2,1)S(1)} %copy-done.2), channel_id=1, source_target_pairs={{0,1},{1,2},{2,3},{3,0},{4,5},{5,6},{6,7},{7,4},{8,9},{9,10},{10,1... | collective-permute-start | bytes 786440 | tf_op jit(solution)/shard_map/ppermute | solution.py:12
  72.4 8.5 %collective-permute-start.1 = (bf16[128,1024]{1,0:T(8,128)(2,1)S(1)}, bf16[128,1024]{1,0:T(8,128)(2,1)S(1)}, u32[]{:S(2)}, u32[]{:S(2)}) collective-permute-start(bf16[128,1024]{1,0:T(8,128)(2,1)S(1)} %collective-permute-done), channel_id=1, source_target_pairs={{0,1},{1,2},{2,3},{3,0},{4,5},{5,6},{6,7},{7,4},{8,9},{9,10},{10,1... | collective-permute-start | bytes 786440 | tf_op jit(solution)/shard_map/ppermute | solution.py:12
  80.9 8.2 %collective-permute-start.2 = (bf16[128,1024]{1,0:T(8,128)(2,1)S(1)}, bf16[128,1024]{1,0:T(8,128)(2,1)S(1)}, u32[]{:S(2)}, u32[]{:S(2)}) collective-permute-start(bf16[128,1024]{1,0:T(8,128)(2,1)S(1)} %collective-permute-done.1), channel_id=1, source_target_pairs={{0,1},{1,2},{2,3},{3,0},{4,5},{5,6},{6,7},{7,4},{8,9},{9,10},{10,1... | collective-permute-start | bytes 786440 | tf_op jit(solution)/shard_map/ppermute | solution.py:12
  80.9 13.9 %copy-start.6 = (bf16[128,1024]{1,0:T(8,128)(2,1)S(1)}, bf16[128,1024]{1,0:T(8,128)(2,1)}, u32[]{:S(2)}) copy-start(bf16[128,1024]{1,0:T(8,128)(2,1)} %param.6) | copy-start | bytes 786436
  94.1 8.8 %copy-start.5 = (bf16[256,1024]{1,0:T(8,128)(2,1)S(1)}, bf16[256,1024]{1,0:T(8,128)(2,1)}, u32[]{:S(2)}) copy-start(bf16[256,1024]{1,0:T(8,128)(2,1)} %copy-done.4) | copy-start | bytes 1572868
Sparse Core Ops, SparseCore 0:
  9.6 30.6 all-gather.1
  64.2 38.6 reduce-scatter.1
  105.2 35.4 all-reduce.1
